TPU v7x, 32 devices: a whole 2x2x4 slice. The times are simulated.
32 devices in a mesh: expert: 8 (over y, x, core), shard: 4 (over z).
Axes of the slice: x: 2, y: 2, z: 4, core: 2. Of those that a mesh axis runs over, the one named last changes fastest.
Arguments:
- inputs: bfloat16 [6304, 768], P(('expert', 'shard')), may hold values from -6 to 6
- routes: int32 [6304, 2], P(('expert', 'shard')), may hold values from 0 to 15, all different within a row; in each aligned block of 197 rows (0 to 196, 197 to 393, ...) at most 39 rows name the same one
- ln1_gain: bfloat16 [768], P(('expert', 'shard')), may hold values from 0.099609375 to 1.8984375
- ln1_bias: bfloat16 [768], P(('expert', 'shard')), may hold values from -3 to 3
- w_qkv: bfloat16 [768, 2304], P(('expert', 'shard')), may hold values from -0.21875 to 0.21875
- w_attn_out: bfloat16 [768, 768], P(('expert', 'shard')), may hold values from -0.625 to 0.625
- ln2_gain: bfloat16 [768], P(('expert', 'shard')), may hold values from 0.099609375 to 1.8984375
- ln2_bias: bfloat16 [768], P(('expert', 'shard')), may hold values from -3 to 3
- w_router: bfloat16 [768, 16], P(('expert', 'shard')), may hold values from -0.109375 to 0.109375
- w_in: bfloat16 [16, 768, 3072], P('expert', None, 'shard'), may hold values from -0.21875 to 0.21875
- w_expert_out: bfloat16 [16, 3072, 768], P('expert', 'shard'), may hold values from -1.25 to 1.25
- cotangent: bfloat16 [6304, 768], P(('expert', 'shard')), may hold values from -6 to 6
Outputs:
- outputs: bfloat16 [6304, 768], P(('expert', 'shard'))
- grad_inputs: float32 [6304, 768], P(('expert', 'shard'))
- grad_ln1_gain: float32 [768], P(('expert', 'shard'))
- grad_ln1_bias: float32 [768], P(('expert', 'shard'))
- grad_w_qkv: float32 [768, 2304], P(('expert', 'shard'))
- grad_w_attn_out: float32 [768, 768], P(('expert', 'shard'))
- grad_ln2_gain: float32 [768], P(('expert', 'shard'))
- grad_ln2_bias: float32 [768], P(('expert', 'shard'))
- grad_w_router: float32 [768, 16], P(('expert', 'shard'))
- grad_w_in: float32 [16, 768, 3072], P('expert', None, 'shard')
- grad_w_expert_out: float32 [16, 3072, 768], P('expert', 'shard')
Inputs may be any that keep to these rules, and one draw needn't show every extreme that they name: `routes`: each token names two different experts; among the 197 tokens of one device no expert is named more than 39 times, and in every draw some expert is named exactly 39 times by one device's tokens.
All inputs are finite; a program needn't handle non-finite values.
Results may differ from a plain program's by a relative error of at most 0.018.
Values may be sent and summed in bfloat16 or wider, within the bound.
No kernel may reach another device: no remote copies, remote signals or barrier semaphores. Data moves between devices by JAX's collectives and lax.ppermute only.
A program may use at most 192 MiB of HBM per device.

v0:
```python
from functools import partial
import jax
import jax.numpy as jnp
from jax import lax
from jax.sharding import PartitionSpec as P

HEADS = 12
HEAD_DIM = 64
EXP_DEV = 2
SEQ = 197
EPS = 1e-06


def layer_norm(values, gain_vec, bias_vec):
    average = jnp.mean(values, axis=-1, keepdims=True)
    centred = values - average
    inverse = lax.rsqrt(jnp.mean(centred * centred, axis=-1, keepdims=True) + EPS)
    unit_vals = centred * inverse
    return (unit_vals * gain_vec + bias_vec, unit_vals, inverse)


def norm_back(grad_out, unit_vals, inverse, gain_vec):
    scaled = grad_out * gain_vec
    centred = (
        scaled
        - jnp.mean(scaled, axis=-1, keepdims=True)
        - unit_vals * jnp.mean(scaled * unit_vals, axis=-1, keepdims=True)
    )
    return (inverse * centred, jnp.sum(grad_out * unit_vals, axis=0), jnp.sum(grad_out, axis=0))


def split_heads(packed):
    shaped = packed.reshape(packed.shape[0], packed.shape[1], 3, HEADS, HEAD_DIM)
    return (shaped[:, :, 0], shaped[:, :, 1], shaped[:, :, 2])


def attn_probs(queries, keys_part):
    scores = jnp.einsum(
        "iqhd,ikhd->ihqk", queries, keys_part, preferred_element_type=jnp.float32
    ) * HEAD_DIM ** (-0.5)
    exponent = jnp.exp(scores)
    return exponent / jnp.sum(exponent, axis=-1, keepdims=True)


def attention_forward(packed):
    queries, keys_part, values_part = split_heads(packed)
    probs_b = attn_probs(queries, keys_part).astype(jnp.bfloat16)
    context = jnp.einsum(
        "ihqk,ikhd->iqhd", probs_b, values_part, preferred_element_type=jnp.float32
    )
    return context.astype(jnp.bfloat16).reshape(packed.shape[0], packed.shape[1], HEADS * HEAD_DIM)


def attention_backward(packed, d_context):
    queries, keys_part, values_part = split_heads(packed)
    probs = attn_probs(queries, keys_part)
    probs_b = probs.astype(jnp.bfloat16)
    d_heads = d_context.reshape(packed.shape[0], packed.shape[1], HEADS, HEAD_DIM)
    d_values = jnp.einsum("ihqk,iqhd->ikhd", probs_b, d_heads, preferred_element_type=jnp.float32)
    d_probs = jnp.einsum(
        "iqhd,ikhd->ihqk", d_heads, values_part, preferred_element_type=jnp.float32
    )
    row_dot = jnp.sum(probs * d_probs, axis=-1, keepdims=True)
    d_scores = (probs * (d_probs - row_dot)).astype(jnp.bfloat16)
    scale = HEAD_DIM ** (-0.5)
    d_queries = (
        jnp.einsum("ihqk,ikhd->iqhd", d_scores, keys_part, preferred_element_type=jnp.float32)
        * scale
    )
    d_keys = (
        jnp.einsum("ihqk,iqhd->ikhd", d_scores, queries, preferred_element_type=jnp.float32) * scale
    )
    stacked = jnp.stack([d_queries, d_keys, d_values], axis=2)
    return stacked.astype(jnp.bfloat16).reshape(
        packed.shape[0], packed.shape[1], 3 * HEADS * HEAD_DIM
    )


def expert_forward(arrived, weight_in, weight_out):
    pre_act = jnp.einsum("emd,edf->emf", arrived, weight_in, preferred_element_type=jnp.float32)
    hidden_act = jax.nn.gelu(pre_act, approximate=True).astype(jnp.bfloat16)
    partial_out = jnp.einsum(
        "emf,efd->emd", hidden_act, weight_out, preferred_element_type=jnp.float32
    )
    return (partial_out, pre_act, hidden_act)


def expert_backward(arrived, grad_rows, pre_act, hidden_act, weight_in, weight_out):
    d_hidden_act = jnp.einsum(
        "emd,efd->emf", grad_rows, weight_out, preferred_element_type=jnp.float32
    )
    _, pullback = jax.vjp(partial(jax.nn.gelu, approximate=True), pre_act)
    d_pre = pullback(d_hidden_act)[0].astype(jnp.bfloat16)
    grad_out_w = jnp.einsum(
        "emf,emd->efd", hidden_act, grad_rows, preferred_element_type=jnp.float32
    )
    grad_in_w = jnp.einsum("emd,emf->edf", arrived, d_pre, preferred_element_type=jnp.float32)
    back_rows = jnp.einsum("emf,edf->emd", d_pre, weight_in, preferred_element_type=jnp.float32)
    return (back_rows, grad_in_w, grad_out_w)


def local(
    inputs,
    routes,
    ln1_gain,
    ln1_bias,
    w_qkv,
    w_attn_out,
    ln2_gain,
    ln2_bias,
    w_router,
    w_in,
    w_expert_out,
    cotangent,
):
    row_count = inputs.shape[0]
    width = inputs.shape[1]
    experts_count = lax.axis_size("expert")
    shard_count = lax.axis_size("shard")
    total_experts = EXP_DEV * experts_count
    capacity = max(2, 16 * row_count // (5 * total_experts))
    images = row_count // SEQ
    (
        full_ln1_gain,
        full_ln1_bias,
        full_qkv,
        full_attn_out,
        full_ln2_gain,
        full_ln2_bias,
        full_router,
    ) = (
        lax.all_gather(ln1_gain, ("expert", "shard"), axis=0, tiled=True),
        lax.all_gather(ln1_bias, ("expert", "shard"), axis=0, tiled=True),
        lax.all_gather(w_qkv, ("expert", "shard"), axis=0, tiled=True),
        lax.all_gather(w_attn_out, ("expert", "shard"), axis=0, tiled=True),
        lax.all_gather(ln2_gain, ("expert", "shard"), axis=0, tiled=True),
        lax.all_gather(ln2_bias, ("expert", "shard"), axis=0, tiled=True),
        lax.all_gather(w_router, ("expert", "shard"), axis=0, tiled=True),
    )
    gain_one = full_ln1_gain.astype(jnp.float32)
    gain_two = full_ln2_gain.astype(jnp.float32)
    features = inputs.astype(jnp.float32)
    normed1, unit_one, inverse_one = layer_norm(
        features, gain_one, full_ln1_bias.astype(jnp.float32)
    )
    narrow_one = normed1.astype(jnp.bfloat16)
    packed = jnp.dot(narrow_one, full_qkv, preferred_element_type=jnp.float32).astype(jnp.bfloat16)
    packed_images = packed.reshape(images, SEQ, 3 * width)
    context = attention_forward(packed_images).reshape(row_count, width)
    hidden = features + jnp.dot(context, full_attn_out, preferred_element_type=jnp.float32)
    normed2, unit_two, inverse_two = layer_norm(hidden, gain_two, full_ln2_bias.astype(jnp.float32))
    narrow_two = normed2.astype(jnp.bfloat16)
    logits = jnp.dot(narrow_two, full_router, preferred_element_type=jnp.float32)
    exponent = jnp.exp(logits)
    router_probs = exponent / jnp.sum(exponent, axis=-1, keepdims=True)
    route_table = (
        routes[:, :, None] == jnp.arange(total_experts, dtype=jnp.int32)[None, None, :]
    ).astype(jnp.float32)
    gate_vals = jnp.sum(route_table * router_probs[:, None, :], axis=-1)
    flat_routes = routes.reshape(-1)
    expert_table = (
        flat_routes[:, None] == jnp.arange(total_experts, dtype=jnp.int32)[None, :]
    ).astype(jnp.int32)
    slot_ranks = jnp.sum((jnp.cumsum(expert_table, axis=0) - 1) * expert_table, axis=1)
    owner_index = flat_routes // EXP_DEV
    local_index = flat_routes % EXP_DEV
    slot_place = (local_index * experts_count + owner_index) * capacity + slot_ranks
    buffer_rows = EXP_DEV * experts_count * capacity
    send_buffer = (
        jnp.zeros((buffer_rows, width), jnp.bfloat16)
        .at[slot_place]
        .set(jnp.repeat(narrow_two, 2, axis=0))
    )
    send_buffer = send_buffer.reshape(EXP_DEV, experts_count, capacity, width)
    copies = jnp.broadcast_to(
        send_buffer[:, :, None], (EXP_DEV, experts_count, shard_count, capacity, width)
    )
    copies = copies.reshape(EXP_DEV, experts_count * shard_count, capacity, width)
    arrived = lax.all_to_all(
        copies, ("expert", "shard"), split_axis=1, concat_axis=1, tiled=True
    ).reshape(EXP_DEV, -1, width)
    partial_out, pre_act, hidden_act = expert_forward(arrived, w_in, w_expert_out)
    returned = lax.all_to_all(
        partial_out.astype(jnp.bfloat16).reshape(
            EXP_DEV, experts_count * shard_count, capacity, width
        ),
        ("expert", "shard"),
        split_axis=1,
        concat_axis=1,
        tiled=True,
    )
    expert_buffer = jnp.sum(
        returned.reshape(EXP_DEV, experts_count, shard_count, capacity, width).astype(jnp.float32),
        axis=2,
    ).astype(jnp.bfloat16)
    expert_vals = (
        expert_buffer.reshape(buffer_rows, width)[slot_place]
        .reshape(row_count, 2, width)
        .astype(jnp.float32)
    )
    outputs = (hidden + jnp.sum(gate_vals[:, :, None] * expert_vals, axis=1)).astype(jnp.bfloat16)
    grad_out = cotangent.astype(jnp.float32)
    d_expert = (
        (gate_vals[:, :, None] * grad_out[:, None, :])
        .astype(jnp.bfloat16)
        .reshape(2 * row_count, width)
    )
    grad_buffer = jnp.zeros((buffer_rows, width), jnp.bfloat16).at[slot_place].set(d_expert)
    grad_buffer = grad_buffer.reshape(EXP_DEV, experts_count, capacity, width)
    grad_copies = jnp.broadcast_to(
        grad_buffer[:, :, None], (EXP_DEV, experts_count, shard_count, capacity, width)
    )
    grad_copies = grad_copies.reshape(EXP_DEV, experts_count * shard_count, capacity, width)
    grad_rows = lax.all_to_all(
        grad_copies, ("expert", "shard"), split_axis=1, concat_axis=1, tiled=True
    ).reshape(EXP_DEV, -1, width)
    back_rows, grad_w_in, grad_w_expert_out = expert_backward(
        arrived, grad_rows, pre_act, hidden_act, w_in, w_expert_out
    )
    back_returned = lax.all_to_all(
        back_rows.astype(jnp.bfloat16).reshape(
            EXP_DEV, experts_count * shard_count, capacity, width
        ),
        ("expert", "shard"),
        split_axis=1,
        concat_axis=1,
        tiled=True,
    )
    back_buffer = jnp.sum(
        back_returned.reshape(EXP_DEV, experts_count, shard_count, capacity, width).astype(
            jnp.float32
        ),
        axis=2,
    ).astype(jnp.bfloat16)
    back_vals = (
        back_buffer.reshape(buffer_rows, width)[slot_place]
        .reshape(row_count, 2, width)
        .astype(jnp.float32)
    )
    d_gate = jnp.sum(expert_vals * grad_out[:, None, :], axis=-1)
    d_probs = jnp.sum(route_table * d_gate[:, :, None], axis=1)
    d_logits = router_probs * (d_probs - jnp.sum(router_probs * d_probs, axis=-1, keepdims=True))
    grad_router = jnp.dot(
        narrow_two.astype(jnp.float32).T, d_logits, precision=lax.Precision.HIGHEST
    )
    d_normed2 = (
        back_vals[:, 0]
        + back_vals[:, 1]
        + jnp.dot(d_logits, full_router.astype(jnp.float32).T, precision=lax.Precision.HIGHEST)
    )
    d_norm_two, grad_gain_two, grad_bias_two = norm_back(d_normed2, unit_two, inverse_two, gain_two)
    d_hidden = grad_out + d_norm_two
    d_hidden_b = d_hidden.astype(jnp.bfloat16)
    grad_attn_out = jnp.dot(context.T, d_hidden_b, preferred_element_type=jnp.float32)
    d_context = jnp.dot(d_hidden_b, full_attn_out.T, preferred_element_type=jnp.float32).astype(
        jnp.bfloat16
    )
    d_packed = attention_backward(packed_images, d_context.reshape(images, SEQ, width)).reshape(
        row_count, 3 * width
    )
    grad_qkv = jnp.dot(narrow_one.T, d_packed, preferred_element_type=jnp.float32)
    d_normed1 = jnp.dot(d_packed, full_qkv.T, preferred_element_type=jnp.float32)
    d_norm_one, grad_gain_one, grad_bias_one = norm_back(d_normed1, unit_one, inverse_one, gain_one)
    grad_inputs = d_hidden + d_norm_one
    shard_grads = (
        lax.psum_scatter(grad_gain_one, ("expert", "shard"), scatter_dimension=0, tiled=True),
        lax.psum_scatter(grad_bias_one, ("expert", "shard"), scatter_dimension=0, tiled=True),
        lax.psum_scatter(grad_qkv, ("expert", "shard"), scatter_dimension=0, tiled=True),
        lax.psum_scatter(grad_attn_out, ("expert", "shard"), scatter_dimension=0, tiled=True),
        lax.psum_scatter(grad_gain_two, ("expert", "shard"), scatter_dimension=0, tiled=True),
        lax.psum_scatter(grad_bias_two, ("expert", "shard"), scatter_dimension=0, tiled=True),
        lax.psum_scatter(grad_router, ("expert", "shard"), scatter_dimension=0, tiled=True),
    )
    return (
        outputs,
        grad_inputs,
        shard_grads[0],
        shard_grads[1],
        shard_grads[2],
        shard_grads[3],
        shard_grads[4],
        shard_grads[5],
        shard_grads[6],
        grad_w_in,
        grad_w_expert_out,
    )


def solution(mesh):
    placed = (
        P(("expert", "shard"), None),
        P(("expert", "shard"), None),
        P(("expert", "shard")),
        P(("expert", "shard")),
        P(("expert", "shard"), None),
        P(("expert", "shard"), None),
        P(("expert", "shard")),
        P(("expert", "shard")),
        P(("expert", "shard"), None),
        P("expert", None, "shard"),
        P("expert", "shard", None),
        P(("expert", "shard"), None),
    )
    return jax.shard_map(
        local,
        mesh=mesh,
        in_specs=placed,
        out_specs=(
            P(("expert", "shard"), None),
            P(("expert", "shard"), None),
            P(("expert", "shard")),
            P(("expert", "shard")),
            P(("expert", "shard"), None),
            P(("expert", "shard"), None),
            P(("expert", "shard")),
            P(("expert", "shard")),
            P(("expert", "shard"), None),
            P("expert", None, "shard"),
            P("expert", "shard", None),
        ),
        check_vma=False,
    )
```

profile of v0, /device:TPU:0, one launch (start us, length us, event | category | flops | bytes accessed | tf_op | source)
XLA Modules:
  0.0 836.1 jit_solution(15612730943233927890)
XLA Ops:
  13.1 42.3 %all-reduce.11 = (bf16[768]{0:T(1024)(128)(2,1)S(1)}, bf16[768]{0:T(1024)(128)(2,1)S(1)}, bf16[768]{0:T(1024)(128)(2,1)S(1)}, bf16[768]{0:T(1024)(128)(2,1)S(1)}) all-reduce(bf16[768]{0:T(1024)(128)(2,1)S(1)} %dynamic-update-slice.1, bf16[768]{0:T(1024)(128)(2,1)S(1)} %dynamic-update-slice, ...), channel_id=1, replica_groups=mesh['expert'=8,'shard'=4] {'expert','shard'}, use_global_device_ids=true, to_apply=%add.2 | all-reduce | flops 3072 | bytes 12288
  60.5 13.1 %all-gather.4.cloned.1.call-done = bf16[768,2304]{1,0:T(8,128)(2,1)} async-done(((bf16[24,2304]{1,0:T(8,128)(2,1)}), bf16[768,2304]{1,0:T(8,128)(2,1)}) %all-gather.4.cloned.1.call-update) | async-done | bytes 3538960 | tf_op jit(solution)/shard_map/all_gather | solution.py:134
  73.6 4.0 convolution_convert_fusion.2
  83.8 45.4 %all-gather.6.cloned.1.call-done = bf16[768,768]{1,0:T(8,128)(2,1)} async-done(((bf16[24,768]{1,0:T(8,128)(2,1)}), bf16[768,768]{1,0:T(8,128)(2,1)}) %all-gather.6.cloned.1.call-update) | async-done | bytes 1179664 | tf_op jit(solution)/shard_map/all_gather | solution.py:135
  152.2 145.9 %all-gather = bf16[32,24,16]{1,2,0:T(8,128)(2,1)S(1)} all-gather(bf16[1,24,16]{1,2,0:T(8,128)(2,1)S(1)} %bitcast.120), channel_id=1, replica_groups=mesh['expert'=8,'shard'=4] {'expert','shard'}, dimensions={0}, use_global_device_ids=true | all-gather | bytes 25344 | tf_op jit(solution)/shard_map/all_gather | solution.py:138
  314.6 5.1 broadcast_in_dim.14
  323.5 6.0 fusion.15
  329.5 4.9 convolution_convert_fusion.1
  334.4 15.0 %copy.145 = bf16[2,1248,768]{2,0,1:T(2,128)(2,1)} copy(bf16[2,1248,768]{2,1,0:T(8,128)(2,1)S(1)} %convolution_convert_fusion.1) | data formatting | bytes 7667712 | tf_op jit(solution)/shard_map/reshape | solution.py:184
  349.5 58.7 %all-to-all-done.2 = bf16[2,32,39,768]{3,0,2,1:T(2,128)(2,1)} async-done(((bf16[2,32,39,768]{3,0,2,1:T(2,128)(2,1)}), bf16[2,32,39,768]{3,0,2,1:T(2,128)(2,1)}, u32[]{:S(2)}, u32[]{:S(2)}) %all-to-all-start.2) | async-done | bytes 3833888 | tf_op jit(solution)/shard_map/all_to_all | solution.py:214
  408.2 5.9 all-to-all-start.1
  414.1 10.3 %fusion.6 = bf16[2,1248,768]{2,1,0:T(8,128)(2,1)S(1)} fusion(f32[2,1248,768]{2,1,0:T(8,128)} %copy-done.28, bf16[2,768,768]{2,1,0:T(8,128)(2,1)S(1)} %copy-done, bf16[2,1248,768]{2,0,1:T(2,128)(2,1)} %bitcast.16), kind=kOutput, calls=%fused_computation.12 | convolution fusion | flops 2982739968 | bytes 17694720 | tf_op jit(solution)/shard_map/emd,efd->emf/dot_general | solution.py:89
  427.9 15.0 %copy.147 = bf16[2,1248,768]{2,0,1:T(2,128)(2,1)} copy(bf16[2,1248,768]{2,1,0:T(8,128)(2,1)S(1)} %convolution_convert_fusion) | data formatting | bytes 7667712 | tf_op jit(solution)/shard_map/reshape | solution.py:221
  443.0 55.8 %all-to-all-done.1 = bf16[2,32,39,768]{3,0,2,1:T(2,128)(2,1)} async-done(((bf16[2,32,39,768]{3,0,2,1:T(2,128)(2,1)}), bf16[2,32,39,768]{3,0,2,1:T(2,128)(2,1)}, u32[]{:S(2)}, u32[]{:S(2)}) %all-to-all-start.1) | async-done | bytes 3833888 | tf_op jit(solution)/shard_map/all_to_all | solution.py:183
  498.8 5.4 all-to-all-start.3
  505.4 6.8 bitcast_reduce_fusion.1
  521.4 67.5 %all-to-all-done.3 = bf16[2,32,39,768]{3,0,2,1:T(2,128)(2,1)} async-done(((bf16[2,32,39,768]{3,0,2,1:T(2,128)(2,1)}), bf16[2,32,39,768]{3,0,2,1:T(2,128)(2,1)}, u32[]{:S(2)}, u32[]{:S(2)}) %all-to-all-start.3) | async-done | bytes 3833888 | tf_op jit(solution)/shard_map/all_to_all | solution.py:220
  588.9 6.8 bitcast_reduce_fusion
  610.6 4.2 fusion.56
  614.8 8.8 %fusion.13 = f32[2,768,768]{2,1,0:T(8,128)} fusion(bf16[2,1248,768]{2,1,0:T(8,128)(2,1)} %copy-done.29, bf16[2,1248,768]{2,0,1:T(2,128)(2,1)} %bitcast.12), kind=kOutput, calls=%fused_computation.23 | convolution fusion | flops 2944401408 | bytes 12386304 | tf_op jit(solution)/shard_map/emd,emf->edf/dot_general | solution.py:97
  623.7 11.5 %fusion.7 = f32[2,768,768]{2,1,0:T(8,128)} fusion(bf16[2,1248,768]{2,0,1:T(2,128)(2,1)} %bitcast.16, f32[2,1248,768]{2,1,0:T(8,128)} %copy-done.28), kind=kOutput, calls=%fused_computation.19 | convolution fusion | flops 2961653760 | bytes 16220160 | tf_op jit(solution)/shard_map/emf,emd->efd/dot_general | solution.py:94
  637.7 42.5 %all-reduce.10 = (f32[768]{0:T(1024)S(1)}, f32[768]{0:T(1024)S(1)}, f32[768]{0:T(1024)S(1)}, f32[768]{0:T(1024)S(1)}, f32[768,16]{0,1:T(8,128)S(1)}) all-reduce(f32[768]{0:T(1024)S(1)} %get-tuple-element.15, f32[768]{0:T(1024)S(1)} %get-tuple-element.20, ...), channel_id=2, replica_groups=mesh['expert'=8,'shard'=4] {'expert','shard'}, use_global_device_ids=true, to_apply=%region_24.25.clone | all-reduce | flops 15360 | bytes 122880
  685.4 19.1 %reduce-scatter.6.cloned.1.call-done = f32[24,768]{1,0:T(8,128)} async-done(((f32[768,768]{1,0:T(8,128)}), f32[24,768]{1,0:T(8,128)}) %reduce-scatter.6.cloned.1.call-update) | async-done | bytes 73744 | tf_op jit(solution)/shard_map/reduce_scatter | solution.py:269
  704.5 124.7 %reduce-scatter.4.cloned.1.call-done = f32[24,2304]{1,0:T(8,128)} async-done(((f32[768,2304]{1,0:T(8,128)}), f32[24,2304]{1,0:T(8,128)}) %reduce-scatter.4.cloned.1.call-update) | async-done | bytes 221200 | tf_op jit(solution)/shard_map/reduce_scatter | solution.py:268
  (163 shorter events, 96.5 us)
Async XLA Ops:
  7.2 322.3 %copy-start = (bf16[2,768,768]{2,1,0:T(8,128)(2,1)S(1)}, bf16[2,768,768]{2,1,0:T(8,128)(2,1)}, u32[]{:S(2)}) copy-start(bf16[2,768,768]{2,1,0:T(8,128)(2,1)} %param.22) | copy-start | bytes 7077892
  7.2 66.4 %all-gather.4.cloned.1.call-start = ((), (), s32[]{:S(2)}) async-start(), calls=%async_computation.6 | async-start | bytes 3649536 | tf_op jit(solution)/shard_map/all_gather | solution.py:134
  7.9 121.2 %all-gather.6.cloned.1.call-start = ((), (), s32[]{:S(2)}) async-start(), calls=%async_computation.7 | async-start | bytes 1216512 | tf_op jit(solution)/shard_map/all_gather | solution.py:135
  59.9 13.7 %copy-start.21 = (f32[197]{0:T(256)}, f32[197]{0:T(256)S(1)}, u32[]{:S(2)}) copy-start(f32[197]{0:T(256)S(1)} %add_rsqrt_fusion.1) | copy-start | bytes 2368
  81.4 47.8 %copy-start.6 = (bf16[197,768]{1,0:T(8,128)(2,1)S(1)}, bf16[197,768]{1,0:T(8,128)(2,1)}, u32[]{:S(2)}) copy-start(bf16[197,768]{1,0:T(8,128)(2,1)} %param.12) | copy-start | bytes 907780
  81.4 50.0 %copy-start.23 = (f32[768]{0:T(1024)S(1)}, f32[768]{0:T(1024)}, u32[]{:S(2)}) copy-start(f32[768]{0:T(1024)} %convert_element_type.112) | copy-start | bytes 9220
  83.8 52.3 %copy-start.24 = (s32[394,1]{0,1:T(1,128)S(1)}, s32[394,1]{0,1:T(1,128)}, u32[]{:S(2)}) copy-start(s32[394,1]{0,1:T(1,128)} %compare_select_fusion) | copy-start | bytes 4732
  148.4 166.2 %all-to-all-start = ((bf16[2,32,39,768]{3,0,2,1:T(2,128)(2,1)}), bf16[2,32,39,768]{3,0,2,1:T(2,128)(2,1)}, u32[]{:S(2)}, u32[]{:S(2)}) async-start(bf16[2,32,39,768]{3,0,2,1:T(2,128)(2,1)} %bitcast.101), calls=%async_computation | async-start | bytes 7667712 | tf_op jit(solution)/shard_map/all_to_all | solution.py:179
  152.1 152.6 %copy-start.20 = (s32[197,2]{0,1:T(2,128)S(1)}, s32[197,2]{0,1:T(2,128)}, u32[]{:S(2)}) copy-start(s32[197,2]{0,1:T(2,128)} %param.13) | copy-start | bytes 4732
  319.7 88.5 %all-to-all-start.2 = ((bf16[2,32,39,768]{3,0,2,1:T(2,128)(2,1)}), bf16[2,32,39,768]{3,0,2,1:T(2,128)(2,1)}, u32[]{:S(2)}, u32[]{:S(2)}) async-start(bf16[2,32,39,768]{3,0,2,1:T(2,128)(2,1)} %bitcast.102), calls=%async_computation.2 | async-start | bytes 7667712 | tf_op jit(solution)/shard_map/all_to_all | solution.py:214
  329.5 4.9 copy-start.28
  408.2 90.6 %all-to-all-start.1 = ((bf16[2,32,39,768]{3,0,2,1:T(2,128)(2,1)}), bf16[2,32,39,768]{3,0,2,1:T(2,128)(2,1)}, u32[]{:S(2)}, u32[]{:S(2)}) async-start(bf16[2,32,39,768]{3,0,2,1:T(2,128)(2,1)} %bitcast.104), calls=%async_computation.1 | async-start | bytes 7667712 | tf_op jit(solution)/shard_map/all_to_all | solution.py:183
  414.1 10.3 %copy-start.27 = (bf16[2,768,768]{2,1,0:T(8,128)(2,1)S(1)}, bf16[2,768,768]{2,1,0:T(8,128)(2,1)}, u32[]{:S(2)}) copy-start(bf16[2,768,768]{2,1,0:T(8,128)(2,1)} %param.21) | copy-start | bytes 7077892
  498.8 5.7 copy-start.14
  498.8 90.1 %all-to-all-start.3 = ((bf16[2,32,39,768]{3,0,2,1:T(2,128)(2,1)}), bf16[2,32,39,768]{3,0,2,1:T(2,128)(2,1)}, u32[]{:S(2)}, u32[]{:S(2)}) async-start(bf16[2,32,39,768]{3,0,2,1:T(2,128)(2,1)} %bitcast.103), calls=%async_computation.3 | async-start | bytes 7667712 | tf_op jit(solution)/shard_map/all_to_all | solution.py:220
  504.3 200.2 %reduce-scatter.6.cloned.1.call-start = ((), (), s32[]{:S(2)}) async-start(), calls=%async_computation.9 | async-start | bytes 2433024 | tf_op jit(solution)/shard_map/reduce_scatter | solution.py:269
  512.5 5.3 copy-start.15
  603.7 225.4 %reduce-scatter.4.cloned.1.call-start = ((), (), s32[]{:S(2)}) async-start(), calls=%async_computation.8 | async-start | bytes 7299072 | tf_op jit(solution)/shard_map/reduce_scatter | solution.py:268
  610.5 4.3 copy-start.11
  623.7 11.5 %copy-start.10 = (bf16[197,768]{1,0:T(8,128)(2,1)S(1)}, bf16[197,768]{1,0:T(8,128)(2,1)}, u32[]{:S(2)}) copy-start(bf16[197,768]{1,0:T(8,128)(2,1)} %copy-done.9) | copy-start | bytes 907780
  623.7 11.8 %copy-start.12 = (bf16[1,197,3,12,64]{1,4,3,2,0:T(8,128)(2,1)S(1)}, bf16[1,197,3,12,64]{1,4,3,2,0:T(8,128)(2,1)}, u32[]{:S(2)}) copy-start(bf16[1,197,3,12,64]{1,4,3,2,0:T(8,128)(2,1)} %copy-done.11) | copy-start | bytes 2723332
  623.7 11.8 %copy-start.26 = (bf16[768,2304]{1,0:T(8,128)(2,1)S(1)}, bf16[768,2304]{1,0:T(8,128)(2,1)}, u32[]{:S(2)}) copy-start(bf16[768,2304]{1,0:T(8,128)(2,1)} %all-gather.4.cloned.1.call-done) | copy-start | bytes 10616836
  635.2 48.0 %copy-start.3 = (f32[197,768]{1,0:T(8,128)S(1)}, f32[197,768]{1,0:T(8,128)}, u32[]{:S(2)}) copy-start(f32[197,768]{1,0:T(8,128)} %copy-done.2) | copy-start | bytes 1815556
  635.2 193.9 %copy-start.1 = (bf16[2,768,768]{2,1,0:T(8,128)(2,1)S(1)}, bf16[2,768,768]{2,1,0:T(8,128)(2,1)}, u32[]{:S(2)}) copy-start(bf16[2,768,768]{2,1,0:T(8,128)(2,1)} %param.22) | copy-start | bytes 7077892
  (14 other events, 29.4 us)
Sparse Core Ops, SparseCore 0:
  10.8 62.7 all-gather.3
  76.4 52.7 all-gather.5
  603.8 100.5 reduce-scatter.5
  710.6 118.5 reduce-scatter.3
where the time goes:
time: 844 us; the launch traced here: 836 us
  waiting for transfers between devices  386 us (46%)
  blocking collectives  231 us (27%)
  local copies, waits for them, and re-layouts  85 us (10%)
  matrix products  69.3 us (8%)
  other arithmetic  31.1 us (4%)
  starting transfers between devices  19.4 us (2%)
  between operations  14.9 us (2%)
    all_gather x1, blocking collectives, local(): lax.all_gather(w_router, ('expert', 'shard'), axis=0, tiled=True)  146 us
    reduce_scatter x1, waiting for transfers between devices, local(): lax.psum_scatter(grad_qkv, ('expert', 'shard'), scatter_dimension=0, tile...  125 us
    unnamed x2, blocking collectives  84.8 us
    all_to_all x1, waiting for transfers between devices, local(): lax.all_to_all(back_rows.astype(jnp.bfloat16).reshape(EXP_DEV, experts_co...  67.5 us
    all_to_all x1, waiting for transfers between devices, local(): lax.all_to_all(grad_copies, ('expert', 'shard'), split_axis=1, concat_axi...  58.7 us
    all_to_all x1, waiting for transfers between devices, local(): lax.all_to_all(partial_out.astype(jnp.bfloat16).reshape(EXP_DEV, experts_...  55.8 us
    all_gather x1, waiting for transfers between devices, local(): lax.all_gather(w_attn_out, ('expert', 'shard'), axis=0, tiled=True)  45.4 us
    reduce_scatter x1, waiting for transfers between devices, local(): lax.psum_scatter(grad_attn_out, ('expert', 'shard'), scatter_dimension=0,...  19.1 us
  transfers between devices with their start and end apart: 8, of which 7 were waited for; matrix products, arithmetic and copies ran while one was open for 17% of the time, Pallas kernels for 0%

commit v1 on v0

--- a/solution.py
+++ b/solution.py
@@ -9,6 +9,29 @@
 EXP_DEV = 2
 SEQ = 197
 EPS = 1e-06
+
+
+def end_columns_over_axis(array_here, row_dim):
+    high = list(array_here.shape[1:])
+    high[row_dim] *= array_here.shape[0]
+    return jnp.moveaxis(array_here, 0, row_dim).reshape(high)
+
+
+def perform_rows(local_array, device_axis):
+    next_value = lax.psum(1, device_axis)
+    carry = lax.axis_index(device_axis)
+    v_next, after = (next_value, carry)
+    everything, right_arr = (local_array[None], 1)
+    while right_arr < v_next:
+        w1 = lax.ppermute(
+            everything, device_axis, [(dev_i, dev_i ^ right_arr) for dev_i in range(v_next)]
+        )
+        arr_next = after & right_arr == 0
+        fresh = jnp.where(arr_next, everything, w1)
+        current_value = jnp.where(arr_next, w1, everything)
+        everything = jnp.concatenate([fresh, current_value])
+        right_arr *= 2
+    return everything
 
 
 def layer_norm(values, gain_vec, bias_vec):
@@ -120,6 +143,11 @@
     total_experts = EXP_DEV * experts_count
     capacity = max(2, 16 * row_count // (5 * total_experts))
     images = row_count // SEQ
+
+    def connect_quarters_now(body, on_dim, vec):
+        spare = perform_rows(vec, body)
+        return end_columns_over_axis(spare, on_dim)
+
     (
         full_ln1_gain,
         full_ln1_bias,
@@ -135,7 +163,7 @@
         lax.all_gather(w_attn_out, ("expert", "shard"), axis=0, tiled=True),
         lax.all_gather(ln2_gain, ("expert", "shard"), axis=0, tiled=True),
         lax.all_gather(ln2_bias, ("expert", "shard"), axis=0, tiled=True),
-        lax.all_gather(w_router, ("expert", "shard"), axis=0, tiled=True),
+        connect_quarters_now(("expert", "shard"), 0, w_router),
     )
     gain_one = full_ln1_gain.astype(jnp.float32)
     gain_two = full_ln2_gain.astype(jnp.float32)

time: 844 us -> 793 us (0.940)
  blocking collectives: 231 us -> 84.7 us
  waiting for transfers between devices: 386 us -> 472 us
  starting transfers between devices: 19.4 us -> 28.1 us
    all_gather x1 -> x0, blocking collectives: 146 us -> none  [local(): lax.all_gather(w_router, ('expert', 'shard'), axis=0, tiled=True)]
    ppermute x0 -> x5, waiting for transfers between devices: none -> 86.1 us  [perform_rows(): lax.ppermute(everything, device_axis, [(dev_i, dev_i ^ right_arr) for dev...]
    ppermute x0 -> x5, starting transfers between devices: none -> 8.68 us  [perform_rows(): lax.ppermute(everything, device_axis, [(dev_i, dev_i ^ right_arr) for dev...]
  transfers between devices with their start and end apart: 8 -> 13, of which waited for: 7 -> 11; matrix products, arithmetic and copies ran while one was open for 17% -> 18% of each run, Pallas kernels for 0% -> 0%
where the time goes in v1:
time: 793 us; the launch traced here: 785 us
  waiting for transfers between devices  472 us (60%)
  local copies, waits for them, and re-layouts  85 us (11%)
  blocking collectives  84.7 us (11%)
  matrix products  69.3 us (9%)
  other arithmetic  31.3 us (4%)
  starting transfers between devices  28.1 us (4%)
  between operations  15 us (2%)
    reduce_scatter x1, waiting for transfers between devices, local(): lax.psum_scatter(grad_qkv, ('expert', 'shard'), scatter_dimension=0, tile...  125 us
    ppermute x5, waiting for transfers between devices, perform_rows(): lax.ppermute(everything, device_axis, [(dev_i, dev_i ^ right_arr) for dev...  86.1 us
    unnamed x2, blocking collectives  84.7 us
    all_to_all x1, waiting for transfers between devices, local(): lax.all_to_all(back_rows.astype(jnp.bfloat16).reshape(EXP_DEV, experts_co...  67.5 us
    all_to_all x1, waiting for transfers between devices, local(): lax.all_to_all(grad_copies, ('expert', 'shard'), split_axis=1, concat_axi...  58.7 us
    all_to_all x1, waiting for transfers between devices, local(): lax.all_to_all(partial_out.astype(jnp.bfloat16).reshape(EXP_DEV, experts_...  55.8 us
    all_gather x1, waiting for transfers between devices, local(): lax.all_gather(w_attn_out, ('expert', 'shard'), axis=0, tiled=True)  45.4 us
    reduce_scatter x1, waiting for transfers between devices, local(): lax.psum_scatter(grad_attn_out, ('expert', 'shard'), scatter_dimension=0,...  19.1 us
  transfers between devices with their start and end apart: 13, of which 11 were waited for; matrix products, arithmetic and copies ran while one was open for 18% of the time, Pallas kernels for 0%

profile of v1, /device:TPU:0, one launch (start us, length us, event | category | flops | bytes accessed | tf_op | source)
XLA Modules:
  0.0 785.3 jit_solution(2768715452736031312)
XLA Ops:
  13.1 42.3 %all-reduce.11 = (bf16[768]{0:T(1024)(128)(2,1)S(1)}, bf16[768]{0:T(1024)(128)(2,1)S(1)}, bf16[768]{0:T(1024)(128)(2,1)S(1)}, bf16[768]{0:T(1024)(128)(2,1)S(1)}) all-reduce(bf16[768]{0:T(1024)(128)(2,1)S(1)} %dynamic-update-slice.1, bf16[768]{0:T(1024)(128)(2,1)S(1)} %dynamic-update-slice, ...), channel_id=1, replica_groups=mesh['expert'=8,'shard'=4] {'expert','shard'}, use_global_device_ids=true, to_apply=%add.2 | all-reduce | flops 3072 | bytes 12288
  60.5 13.1 %all-gather.3.cloned.1.call-done = bf16[768,2304]{1,0:T(8,128)(2,1)} async-done(((bf16[24,2304]{1,0:T(8,128)(2,1)}), bf16[768,2304]{1,0:T(8,128)(2,1)}) %all-gather.3.cloned.1.call-update) | async-done | bytes 3538960 | tf_op jit(solution)/shard_map/all_gather | solution.py:162
  83.8 45.4 %all-gather.5.cloned.1.call-done = bf16[768,768]{1,0:T(8,128)(2,1)} async-done(((bf16[24,768]{1,0:T(8,128)(2,1)}), bf16[768,768]{1,0:T(8,128)(2,1)}) %all-gather.5.cloned.1.call-update) | async-done | bytes 1179664 | tf_op jit(solution)/shard_map/all_gather | solution.py:163
  153.9 61.2 %collective-permute-done = bf16[1,24,16]{1,2,0:T(8,128)(2,1)S(1)} collective-permute-done((bf16[1,24,16]{1,2,0:T(8,128)(2,1)S(1)}, bf16[1,24,16]{1,2,0:T(8,128)(2,1)S(1)}, u32[]{:S(2)}, u32[]{:S(2)}) %collective-permute-start) | collective-permute-done | bytes 800 | tf_op jit(solution)/shard_map/ppermute | solution.py:26
  215.1 5.3 collective-permute-start.1
  220.4 19.9 %collective-permute-done.1 = bf16[2,24,16]{1,2,0:T(8,128)(2,1)S(1)} collective-permute-done((bf16[2,24,16]{1,2,0:T(8,128)(2,1)S(1)}, bf16[2,24,16]{1,2,0:T(8,128)(2,1)S(1)}, u32[]{:S(2)}, u32[]{:S(2)}) %collective-permute-start.1) | collective-permute-done | bytes 1568 | tf_op jit(solution)/shard_map/ppermute | solution.py:26
  263.8 5.1 broadcast_in_dim.17
  272.7 6.0 fusion.15
  278.7 4.9 convolution_convert_fusion.1
  283.6 15.0 %copy.145 = bf16[2,1248,768]{2,0,1:T(2,128)(2,1)} copy(bf16[2,1248,768]{2,1,0:T(8,128)(2,1)S(1)} %convolution_convert_fusion.1) | data formatting | bytes 7667712 | tf_op jit(solution)/shard_map/reshape | solution.py:212
  298.6 58.7 %all-to-all-done.2 = bf16[2,32,39,768]{3,0,2,1:T(2,128)(2,1)} async-done(((bf16[2,32,39,768]{3,0,2,1:T(2,128)(2,1)}), bf16[2,32,39,768]{3,0,2,1:T(2,128)(2,1)}, u32[]{:S(2)}, u32[]{:S(2)}) %all-to-all-start.2) | async-done | bytes 3833888 | tf_op jit(solution)/shard_map/all_to_all | solution.py:242
  357.4 5.9 all-to-all-start.1
  363.3 10.3 %fusion.6 = bf16[2,1248,768]{2,1,0:T(8,128)(2,1)S(1)} fusion(f32[2,1248,768]{2,1,0:T(8,128)} %copy-done.28, bf16[2,768,768]{2,1,0:T(8,128)(2,1)S(1)} %copy-done, bf16[2,1248,768]{2,0,1:T(2,128)(2,1)} %bitcast.16), kind=kOutput, calls=%fused_computation.12 | convolution fusion | flops 2982739968 | bytes 17694720 | tf_op jit(solution)/shard_map/emd,efd->emf/dot_general | solution.py:112
  377.1 15.0 %copy.147 = bf16[2,1248,768]{2,0,1:T(2,128)(2,1)} copy(bf16[2,1248,768]{2,1,0:T(8,128)(2,1)S(1)} %convolution_convert_fusion) | data formatting | bytes 7667712 | tf_op jit(solution)/shard_map/reshape | solution.py:249
  392.1 55.8 %all-to-all-done.1 = bf16[2,32,39,768]{3,0,2,1:T(2,128)(2,1)} async-done(((bf16[2,32,39,768]{3,0,2,1:T(2,128)(2,1)}), bf16[2,32,39,768]{3,0,2,1:T(2,128)(2,1)}, u32[]{:S(2)}, u32[]{:S(2)}) %all-to-all-start.1) | async-done | bytes 3833888 | tf_op jit(solution)/shard_map/all_to_all | solution.py:211
  448.0 5.4 all-to-all-start.3
  454.5 6.8 bitcast_reduce_fusion.1
  470.6 67.5 %all-to-all-done.3 = bf16[2,32,39,768]{3,0,2,1:T(2,128)(2,1)} async-done(((bf16[2,32,39,768]{3,0,2,1:T(2,128)(2,1)}), bf16[2,32,39,768]{3,0,2,1:T(2,128)(2,1)}, u32[]{:S(2)}, u32[]{:S(2)}) %all-to-all-start.3) | async-done | bytes 3833888 | tf_op jit(solution)/shard_map/all_to_all | solution.py:248
  538.1 6.8 bitcast_reduce_fusion
  564.0 8.8 %fusion.13 = f32[2,768,768]{2,1,0:T(8,128)} fusion(bf16[2,1248,768]{2,1,0:T(8,128)(2,1)} %copy-done.29, bf16[2,1248,768]{2,0,1:T(2,128)(2,1)} %bitcast.12), kind=kOutput, calls=%fused_computation.23 | convolution fusion | flops 2944401408 | bytes 12386304 | tf_op jit(solution)/shard_map/emd,emf->edf/dot_general | solution.py:120
  572.8 11.5 %fusion.7 = f32[2,768,768]{2,1,0:T(8,128)} fusion(bf16[2,1248,768]{2,0,1:T(2,128)(2,1)} %bitcast.16, f32[2,1248,768]{2,1,0:T(8,128)} %copy-done.28), kind=kOutput, calls=%fused_computation.19 | convolution fusion | flops 2961653760 | bytes 16220160 | tf_op jit(solution)/shard_map/emf,emd->efd/dot_general | solution.py:117
  586.8 42.5 %all-reduce.10 = (f32[768]{0:T(1024)S(1)}, f32[768]{0:T(1024)S(1)}, f32[768]{0:T(1024)S(1)}, f32[768]{0:T(1024)S(1)}, f32[768,16]{0,1:T(8,128)S(1)}) all-reduce(f32[768]{0:T(1024)S(1)} %get-tuple-element.15, f32[768]{0:T(1024)S(1)} %get-tuple-element.20, ...), channel_id=2, replica_groups=mesh['expert'=8,'shard'=4] {'expert','shard'}, use_global_device_ids=true, to_apply=%region_24.25.clone | all-reduce | flops 15360 | bytes 122880
  634.5 19.1 %reduce-scatter.6.cloned.1.call-done = f32[24,768]{1,0:T(8,128)} async-done(((f32[768,768]{1,0:T(8,128)}), f32[24,768]{1,0:T(8,128)}) %reduce-scatter.6.cloned.1.call-update) | async-done | bytes 73744 | tf_op jit(solution)/shard_map/reduce_scatter | solution.py:297
  653.6 124.7 %reduce-scatter.4.cloned.1.call-done = f32[24,2304]{1,0:T(8,128)} async-done(((f32[768,2304]{1,0:T(8,128)}), f32[24,2304]{1,0:T(8,128)}) %reduce-scatter.4.cloned.1.call-update) | async-done | bytes 221200 | tf_op jit(solution)/shard_map/reduce_scatter | solution.py:296
  (182 shorter events, 113.4 us)
Async XLA Ops:
  7.2 271.5 %copy-start = (bf16[2,768,768]{2,1,0:T(8,128)(2,1)S(1)}, bf16[2,768,768]{2,1,0:T(8,128)(2,1)}, u32[]{:S(2)}) copy-start(bf16[2,768,768]{2,1,0:T(8,128)(2,1)} %param.22) | copy-start | bytes 7077892
  7.2 66.4 %all-gather.3.cloned.1.call-start = ((), (), s32[]{:S(2)}) async-start(), calls=%async_computation.6 | async-start | bytes 3649536 | tf_op jit(solution)/shard_map/all_gather | solution.py:162
  7.9 121.2 %all-gather.5.cloned.1.call-start = ((), (), s32[]{:S(2)}) async-start(), calls=%async_computation.7 | async-start | bytes 1216512 | tf_op jit(solution)/shard_map/all_gather | solution.py:163
  59.9 13.7 %copy-start.21 = (f32[197]{0:T(256)}, f32[197]{0:T(256)S(1)}, u32[]{:S(2)}) copy-start(f32[197]{0:T(256)S(1)} %add_rsqrt_fusion.1) | copy-start | bytes 2368
  81.4 47.8 %copy-start.6 = (bf16[197,768]{1,0:T(8,128)(2,1)S(1)}, bf16[197,768]{1,0:T(8,128)(2,1)}, u32[]{:S(2)}) copy-start(bf16[197,768]{1,0:T(8,128)(2,1)} %param.12) | copy-start | bytes 907780
  81.4 50.0 %copy-start.23 = (f32[768]{0:T(1024)S(1)}, f32[768]{0:T(1024)}, u32[]{:S(2)}) copy-start(f32[768]{0:T(1024)} %convert_element_type.112) | copy-start | bytes 9220
  83.8 52.3 %copy-start.24 = (s32[394,1]{0,1:T(1,128)S(1)}, s32[394,1]{0,1:T(1,128)}, u32[]{:S(2)}) copy-start(s32[394,1]{0,1:T(1,128)} %compare_select_fusion) | copy-start | bytes 4732
  148.5 115.3 %all-to-all-start = ((bf16[2,32,39,768]{3,0,2,1:T(2,128)(2,1)}), bf16[2,32,39,768]{3,0,2,1:T(2,128)(2,1)}, u32[]{:S(2)}, u32[]{:S(2)}) async-start(bf16[2,32,39,768]{3,0,2,1:T(2,128)(2,1)} %bitcast.103), calls=%async_computation | async-start | bytes 7667712 | tf_op jit(solution)/shard_map/all_to_all | solution.py:207
  152.2 101.8 %copy-start.20 = (s32[197,2]{0,1:T(2,128)S(1)}, s32[197,2]{0,1:T(2,128)}, u32[]{:S(2)}) copy-start(s32[197,2]{0,1:T(2,128)} %param.13) | copy-start | bytes 4732
  152.2 62.9 %collective-permute-start = (bf16[1,24,16]{1,2,0:T(8,128)(2,1)S(1)}, bf16[1,24,16]{1,2,0:T(8,128)(2,1)S(1)}, u32[]{:S(2)}, u32[]{:S(2)}) collective-permute-start(bf16[1,24,16]{1,2,0:T(8,128)(2,1)S(1)} %bitcast.122), channel_id=1, source_target_pairs={{0,1},{1,0},{2,3},{3,2},{4,5},{5,4},{6,7},{7,6},{8,9},{9,8},{10,11... | collective-permute-start | bytes 2312 | tf_op jit(solution)/shard_map/ppermute | solution.py:26
  215.1 25.1 %collective-permute-start.1 = (bf16[2,24,16]{1,2,0:T(8,128)(2,1)S(1)}, bf16[2,24,16]{1,2,0:T(8,128)(2,1)S(1)}, u32[]{:S(2)}, u32[]{:S(2)}) collective-permute-start(bf16[2,24,16]{1,2,0:T(8,128)(2,1)S(1)} %pad_maximum_fusion.5), channel_id=1, source_target_pairs={{0,2},{1,3},{2,0},{3,1},{4,6},{5,7},{6,4},{7,5},{8,10},{9,11},{10,... | collective-permute-start | bytes 4616 | tf_op jit(solution)/shard_map/ppermute | solution.py:26
  240.3 1.2 collective-permute-start.2
  241.5 4.0 collective-permute-start.3
  245.6 6.8 collective-permute-start.4
  268.9 88.5 %all-to-all-start.2 = ((bf16[2,32,39,768]{3,0,2,1:T(2,128)(2,1)}), bf16[2,32,39,768]{3,0,2,1:T(2,128)(2,1)}, u32[]{:S(2)}, u32[]{:S(2)}) async-start(bf16[2,32,39,768]{3,0,2,1:T(2,128)(2,1)} %bitcast.104), calls=%async_computation.2 | async-start | bytes 7667712 | tf_op jit(solution)/shard_map/all_to_all | solution.py:242
  357.4 90.6 %all-to-all-start.1 = ((bf16[2,32,39,768]{3,0,2,1:T(2,128)(2,1)}), bf16[2,32,39,768]{3,0,2,1:T(2,128)(2,1)}, u32[]{:S(2)}, u32[]{:S(2)}) async-start(bf16[2,32,39,768]{3,0,2,1:T(2,128)(2,1)} %bitcast.106), calls=%async_computation.1 | async-start | bytes 7667712 | tf_op jit(solution)/shard_map/all_to_all | solution.py:211
  448.0 90.1 %all-to-all-start.3 = ((bf16[2,32,39,768]{3,0,2,1:T(2,128)(2,1)}), bf16[2,32,39,768]{3,0,2,1:T(2,128)(2,1)}, u32[]{:S(2)}, u32[]{:S(2)}) async-start(bf16[2,32,39,768]{3,0,2,1:T(2,128)(2,1)} %bitcast.105), calls=%async_computation.3 | async-start | bytes 7667712 | tf_op jit(solution)/shard_map/all_to_all | solution.py:248
  453.4 200.2 %reduce-scatter.6.cloned.1.call-start = ((), (), s32[]{:S(2)}) async-start(), calls=%async_computation.9 | async-start | bytes 2433024 | tf_op jit(solution)/shard_map/reduce_scatter | solution.py:297
  552.9 225.4 %reduce-scatter.4.cloned.1.call-start = ((), (), s32[]{:S(2)}) async-start(), calls=%async_computation.8 | async-start | bytes 7299072 | tf_op jit(solution)/shard_map/reduce_scatter | solution.py:296
  572.8 11.5 %copy-start.10 = (bf16[197,768]{1,0:T(8,128)(2,1)S(1)}, bf16[197,768]{1,0:T(8,128)(2,1)}, u32[]{:S(2)}) copy-start(bf16[197,768]{1,0:T(8,128)(2,1)} %copy-done.9) | copy-start | bytes 907780
  572.8 11.8 %copy-start.12 = (bf16[1,197,3,12,64]{1,4,3,2,0:T(8,128)(2,1)S(1)}, bf16[1,197,3,12,64]{1,4,3,2,0:T(8,128)(2,1)}, u32[]{:S(2)}) copy-start(bf16[1,197,3,12,64]{1,4,3,2,0:T(8,128)(2,1)} %copy-done.11) | copy-start | bytes 2723332
  572.8 11.8 %copy-start.26 = (bf16[768,2304]{1,0:T(8,128)(2,1)S(1)}, bf16[768,2304]{1,0:T(8,128)(2,1)}, u32[]{:S(2)}) copy-start(bf16[768,2304]{1,0:T(8,128)(2,1)} %all-gather.3.cloned.1.call-done) | copy-start | bytes 10616836
  584.4 48.0 %copy-start.3 = (f32[197,768]{1,0:T(8,128)S(1)}, f32[197,768]{1,0:T(8,128)}, u32[]{:S(2)}) copy-start(f32[197,768]{1,0:T(8,128)} %copy-done.2) | copy-start | bytes 1815556
  584.4 193.9 %copy-start.1 = (bf16[2,768,768]{2,1,0:T(8,128)(2,1)S(1)}, bf16[2,768,768]{2,1,0:T(8,128)(2,1)}, u32[]{:S(2)}) copy-start(bf16[2,768,768]{2,1,0:T(8,128)(2,1)} %param.22) | copy-start | bytes 7077892
  (19 other events, 59.8 us)
Sparse Core Ops, SparseCore 0:
  10.8 62.7 all-gather.2
  76.4 52.7 all-gather.4
  553.0 100.5 reduce-scatter.5
  659.7 118.5 reduce-scatter.3
